TPU v7x, 128 devices: a whole 4x4x4 slice. The times are simulated.
128 devices in a mesh: tm: 32 (over z, y, x_hi), clip: 4 (over x_lo, core).
Axes of the slice: x: 4 (x_hi: 2, x_lo: 2; x = x_hi * 2 + x_lo), y: 4, z: 4, core: 2. Of those that a mesh axis runs over, the one named last changes fastest.
Arguments:
- student_query: bfloat16 [16384, 1024], P('tm', 'clip'), may hold values from -12 to 12
- teacher_key: bfloat16 [65536, 1024], P('tm', 'clip'), may hold values from -1000 to 1000
- teacher_value: bfloat16 [65536, 1024], P('tm', 'clip'), may hold values from -12 to 12
- clip_order: int32 [65536], replicated, may hold values from 0 to 65535, as said below
- band_start: int32 [512], P('tm'), may hold values from -16 to -1
- band_end: int32 [512], P('tm'), may hold values from 1 to 16
- output_weight: bfloat16 [1024, 1024], P('clip'), may hold values from -0.1875 to 0.1875
- cotangent: bfloat16 [16384, 1024], P('tm', 'clip'), may hold values from -6 to 6
Outputs:
- joined: bfloat16 [16384, 1024], P('tm', 'clip')
- grad_query: bfloat16 [16384, 1024], P('tm', 'clip')
- grad_output_weight: float32 [1024, 1024], P('clip')
Inputs may be any that keep to these rules, and one draw needn't show every extreme that they name: clip_order is a permutation. For a time row t of time shard j = t // 2048, clip_order[t] % 2048 lies in [j * 64, (j + 1) * 64): every input shard holds exactly 64 rows of every time shard, as one run.
All inputs are finite; a program needn't handle non-finite values.
Results may differ from a plain program's by a relative error of at most 0.0094.
Values may be sent and summed in bfloat16 or wider, within the bound.
A program may use at most 128 MiB of HBM per device.

v0:
```python
import functools
import math

import jax
import jax.numpy as jnp
from jax import lax
from jax.experimental import pallas as pl
from jax.experimental.pallas import tpu as pltpu
from jax.sharding import PartitionSpec as P

HDIM = 64
SBLK = 32
TBLK = 128
F = 128
CH = 1536
SUB = 512
GROUP = 1024
FAR = -3e38
ANY = pl.BlockSpec(memory_space=pl.ANY)
MESH = pl.DeviceIdType.MESH


def greet(shards, bits, wait=True):
    me = lax.axis_index("tm")
    c = lax.axis_index("clip")
    barrier = pltpu.get_barrier_semaphore()

    def tell(d, carry):
        pl.semaphore_signal(
            barrier, inc=1, device_id={"tm": lax.rem(me + d, shards)}, device_id_type=MESH
        )
        return carry

    lax.fori_loop(1, shards, tell, 0)
    for bit in bits:
        pl.semaphore_signal(
            barrier, inc=1, device_id={"clip": flip(c, bit)}, device_id_type=MESH
        )
    if wait:
        pl.semaphore_wait(barrier, shards - 1 + len(bits))


def flip(c, bit):
    if bit == 3:
        return 3 - c
    return c + bit - 2 * bit * lax.rem(lax.div(c, bit), 2)


def one_hot_rows(row, hot, at, side, piece):
    lane = lax.broadcasted_iota(jnp.int32, (128, 128), 1)
    col = jnp.broadcast_to(row, (128, 128)).T
    spot = lax.div(col, side) * piece + lax.rem(col, piece)
    base = jnp.where(lax.rem(spot, 128) == lane, lax.div(spot, 128), -1)
    base = base.astype(jnp.float32).astype(jnp.bfloat16)
    one = jnp.bfloat16(1)
    for k in range(side // 128):
        hot[at : at + 128, k * 128 : (k + 1) * 128] = jnp.maximum(
            one - jnp.abs(base - jnp.bfloat16(k)), jnp.bfloat16(0)
        )


def send(src, dst, sems, **where):
    return pltpu.make_async_remote_copy(
        src_ref=src, dst_ref=dst, send_sem=sems[0], recv_sem=sems[1],
        device_id=where, device_id_type=MESH,
    )


def step_kernel(
    shards, tiles, tk, tv, sq, cot, ow, starts, ends, order,
    joined, dq, wsum,
    kvin, left, right, idx, hot, kv, kvt, s0, s1, d0, d1, d2, p0, p1, qb, gb,
    cotv, wv, wcols, gv, qp, gp, bv, bp, band,
    o_send, dq_send, dq_own, og, wg, got, red,
    ks, kr, vs, vr, ls, lr, rs, rr, ss, sr, gs, gr,
    oss, osr, dss, dsr, ws, wr, cs, ms, fs, os_,
):
    f32 = jnp.float32
    bf = jnp.bfloat16
    me = lax.axis_index("tm")
    c = lax.axis_index("clip")
    half = lax.rem(me, 2)
    mate = flip(me, 1)
    pair = lax.div(me, 2)
    groups, rows_here, wide = cotv.shape
    near, far = flip(c, 1), flip(c, 2)
    prev = lax.rem(me + shards - 2, shards)
    after = lax.rem(me + 2, shards)
    L = 2 * F
    nb = F // SBLK
    per = CH // TBLK
    piece = tk.shape[1]
    side = shards * piece
    irows = side // 128
    blocks = F * tiles // SBLK
    half_blocks = blocks // 2
    half_tiles = tiles // 2
    reach = side // TBLK
    span = (2 * reach + nb) // per
    scores, dprobs, weights = (s0, s1), (d0, d1, d2), (p0, p1)
    part_rows, part_cols = red.shape
    own_cols = pl.ds(pl.multiple_of(half * 128, 128), 128)
    mate_cols = pl.ds(pl.multiple_of((1 - half) * 128, 128), 128)
    bv[...] = jnp.zeros_like(bv)
    bv[0:1, 0:half_blocks] = starts[...]
    bv[1:2, 0:half_blocks] = ends[...]
    greet(shards, (1, 2, 3))

    def key_copies(target, slot, src):
        p = lax.div(target, 2)
        col = pl.multiple_of(lax.rem(target, 2) * 128, 128)
        return (
            send(
                tk.at[pl.ds(2 * p, 2), :, pl.ds(col, 128)],
                kvin.at[:, me, :, pl.ds(0, 128)], (ks.at[slot], kr.at[src]), tm=target,
            ),
            send(
                tv.at[pl.ds(2 * p, 2), :, pl.ds(col, 128)],
                kvin.at[:, me, :, pl.ds(128, 128)], (vs.at[slot], vr.at[src]), tm=target,
            ),
        )

    def halo_copies(s):
        return (
            send(kvin.at[0, s], right.at[s], (rs.at[s], rr.at[s]), tm=prev),
            send(kvin.at[1, s], left.at[s], (ls.at[s], lr.at[s]), tm=after),
        )

    def w_copy(d, src):
        target = lax.rem(c + d, groups)
        theirs = pl.multiple_of(target * wide, 128)
        return send(
            ow.at[:, pl.ds(theirs, wide)], wcols.at[c], (ws.at[d], wr.at[src]), clip=target
        )

    mine = pl.multiple_of(c * wide, 128)
    cot_far = send(cot, cotv.at[c], (cs.at[0], cs.at[1]), clip=far)
    cot_near = send(cot, cotv.at[c], (cs.at[2], cs.at[3]), clip=near)
    cot_relay = send(cotv.at[far], cotv.at[far], (cs.at[4], cs.at[5]), clip=near)
    q_copy = send(sq.at[:, mate_cols], qp.at[half], (ms.at[0], ms.at[1]), tm=mate)
    b_copy = send(bv, bp.at[half], (ms.at[2], ms.at[3]), tm=mate)
    g_copy = send(gv.at[1 - half], gp.at[half], (ms.at[4], ms.at[5]), tm=mate)

    cot_far.start()
    cot_near.start()

    def start_keys(d, carry):
        for copy in key_copies(lax.rem(me + d, shards), d, me):
            copy.start()
        return carry

    lax.fori_loop(1, shards, start_keys, 0)
    q_copy.start()
    b_copy.start()
    mine_kv = (
        pltpu.make_async_copy(
            tk.at[pl.ds(2 * pair, 2), :, own_cols], kvin.at[:, me, :, pl.ds(0, 128)], os_.at[0]
        ),
        pltpu.make_async_copy(
            tv.at[pl.ds(2 * pair, 2), :, own_cols], kvin.at[:, me, :, pl.ds(128, 128)], os_.at[1]
        ),
    )
    mine_cot = (
        pltpu.make_async_copy(cot, cotv.at[c], os_.at[2]),
        pltpu.make_async_copy(ow, wv, os_.at[3]),
    )
    get_idx = []
    for e in range(4):
        at = pl.multiple_of(lax.rem(2 * pair + shards - 1 + e, shards) * irows, irows)
        get_idx.append(
            pltpu.make_async_copy(
                order.at[pl.ds(at, irows)], idx.at[pl.ds(e * irows, irows)], os_.at[7 + e]
            )
        )
    mine_rest = (
        pltpu.make_async_copy(ow.at[:, pl.ds(mine, wide)], wcols.at[c], os_.at[4]),
        pltpu.make_async_copy(sq.at[:, own_cols], qp.at[half], os_.at[5]),
        pltpu.make_async_copy(bv, bp.at[half], os_.at[6]),
    ) + tuple(get_idx)
    for copy in mine_cot + mine_kv + mine_rest:
        copy.start()
    for copy in mine_cot + mine_kv:
        copy.wait()
    for copy in halo_copies(me):
        copy.start()
    cot_far.wait_recv()
    cot_relay.start()
    cot_near.wait_recv()
    cot_relay.wait_recv()
    nt = (((1,), (1,)), ((), ()))
    grad = jnp.zeros((rows_here, wide), f32)
    for j in range(groups):
        grad += lax.dot_general(
            cotv[j], wv[:, j * wide : (j + 1) * wide], nt, preferred_element_type=f32
        )
    gv[0] = grad[:, 0:128].astype(bf)
    gv[1] = grad[:, 128:256].astype(bf)

    def forward(d, carry):
        s = lax.rem(me + shards - d, shards)
        for copy in key_copies(lax.rem(me + d, shards), d, s):
            copy.wait_recv()
        for copy in halo_copies(s):
            copy.start()
        return carry

    lax.fori_loop(1, 3, forward, 0)
    g_copy.start()
    put_g = pltpu.make_async_copy(gv.at[half], gp.at[half], os_.at[11])
    put_g.start()
    for copy in mine_rest:
        copy.wait()
    kvt[256:272, :] = jnp.ones((16, kvt.shape[1]), bf)
    lane = lax.broadcasted_iota(jnp.int32, (128, 128), 1)

    def mark(k, carry):
        at = pl.multiple_of(k * TBLK, TBLK)
        kv[pl.ds(at, TBLK), 128:256] = jnp.where(lane == k, 1.0, 0.0).astype(bf)
        return carry

    lax.fori_loop(0, 4 * reach, mark, 0)
    lax.fori_loop(3, shards, forward, 0)
    for d in range(1, groups):
        w_copy(d, c).start()

    def place(src, first, j):
        for r in range(GROUP // 128):
            row = lax.div(first, 128) + j * (GROUP // 128) + r
            one_hot_rows(idx[pl.ds(row, 1), :], hot, r * 128, side, piece)
        rows = jnp.dot(hot[...], src.reshape(side, 256), preferred_element_type=f32).astype(bf)
        at = pl.multiple_of(first + j * GROUP, GROUP)
        kv[pl.ds(at, GROUP), 0:128] = rows[:, 0:128]
        kv[pl.ds(at, GROUP), 256:384] = rows[:, 128:256]
        kvt[0:256, pl.ds(at, GROUP)] = rows.T

    def sort_own(j, carry):
        place(kvin[lax.div(j * GROUP, side)], side, j)
        return carry

    def sort_left(j, carry):
        place(left[...], 0, j)
        return carry

    def sort_right(j, carry):
        place(right[...], 3 * side, j)
        return carry

    lax.fori_loop(0, 2 * side // GROUP, sort_own, 0)
    q_copy.wait_recv()
    b_copy.wait_recv()
    g_copy.wait_recv()
    put_g.wait()
    get_band = pltpu.make_async_copy(bp, band, os_.at[12])
    get_band.start()
    get_band.wait()

    def came_left(s, carry):
        halo_copies(s)[1].wait_recv()
        return carry

    def came_right(s, carry):
        halo_copies(s)[0].wait_recv()
        return carry

    lax.fori_loop(0, shards, came_left, 0)
    lax.fori_loop(0, side // GROUP, sort_left, 0)
    lax.fori_loop(0, shards, came_right, 0)
    lax.fori_loop(0, side // GROUP, sort_right, 0)

    flane = lax.broadcasted_iota(jnp.int32, (F, 128), 1)
    zero = jnp.zeros((F, 128), bf)
    tops, deltas, invs = {}, {}, {}

    def tile_at(t):
        return lax.rem(t + (1 - half) * half_tiles, tiles)

    def frames(ref, t):
        at = pl.multiple_of(lax.rem(tile_at(t), half_tiles) * F, F)
        return ref[lax.div(tile_at(t), half_tiles), pl.ds(at, F), :]

    def split_heads(x):
        return jnp.where(flane < HDIM, x, zero), jnp.where(flane < HDIM, zero, x)

    def join_heads(x):
        x = x.T
        return jnp.where(flane < HDIM, x[0:F], x[F:L])

    def spot(t, k, u):
        return pl.multiple_of(tile_at(t) * (nb * TBLK) + k * CH + u * SUB, TBLK)

    def o_copy(t):
        part = pl.ds(t * F, F)
        return send(
            o_send.at[part], og.at[c, part, own_cols], (oss.at[t], osr.at[t]), tm=mate
        )

    def dq_copy(t):
        part = pl.ds(t * F, F)
        return send(
            dq_send.at[part], dq.at[part, own_cols], (dss.at[t], dsr.at[t]), tm=mate
        )

    for t in range(tiles + 2):
        do1, do2, do3 = t < tiles, 1 <= t <= tiles, t >= 2
        if do1:
            q = frames(qp, t) * bf(1.0 / math.sqrt(HDIM))
            qb[0:F, 0:128], qb[F:L, 0:128] = split_heads(q)
            gb[0:F, :], gb[F:L, :] = split_heads(frames(gp, t))
            block = lax.broadcasted_iota(jnp.int32, (SBLK, 128), 1)
            row = lax.div(tile_at(t), half_tiles)
            col = lax.rem(tile_at(t), half_tiles) * nb
            base_block = pair * blocks
            for r in range(nb):
                at = reach + tile_at(t) * nb + r
                lo = jnp.maximum(at + band[row, 0, col + r], reach - base_block)
                hi = jnp.minimum(
                    at + band[row, 1, col + r], shards * half_blocks - 1 + reach - base_block
                )
                bias = jnp.where((block >= lo) & (block <= hi), 0.0, FAR).astype(bf)
                qb[r * SBLK : (r + 1) * SBLK, 128:256] = bias
                qb[F + r * SBLK : F + (r + 1) * SBLK, 128:256] = bias

        def body(k, carry):
            top, o, dqt = carry
            for u in range(CH // SUB):
                at = pl.multiple_of(k * CH + u * SUB, SUB)
                if do1:
                    base = spot(t, k, u)
                    s = lax.dot_general(
                        kv[pl.ds(base, SUB), 0:256], qb[...], nt, preferred_element_type=f32
                    )
                    dprobs[t % 3][pl.ds(at, SUB), :] = lax.dot_general(
                        kv[pl.ds(base, SUB), 256:384], gb[...], nt, preferred_element_type=f32
                    )
                    scores[t % 2][pl.ds(at, SUB), :] = s
                    top = jnp.maximum(top, jnp.max(s.reshape(SUB // 8, 8, L), axis=0))
                if do2:
                    base = spot(t - 1, k, u)
                    s = scores[(t - 1) % 2][pl.ds(at, SUB), :].reshape(SUB // 8, 8, L)
                    e = jnp.exp(s - tops[t - 1][None]).reshape(SUB, L).astype(bf)
                    weights[(t - 1) % 2][pl.ds(at, SUB), :] = e
                    o = o + jnp.dot(kvt[128:272, pl.ds(base, SUB)], e, preferred_element_type=f32)
                if do3:
                    base = spot(t - 2, k, u)
                    e = weights[t % 2][pl.ds(at, SUB), :].astype(f32).reshape(SUB // 8, 8, L)
                    d = dprobs[(t - 2) % 3][pl.ds(at, SUB), :].reshape(SUB // 8, 8, L)
                    ds = (e * (d - deltas[t - 2][None])).reshape(SUB, L).astype(bf)
                    dqt = dqt + jnp.dot(
                        kvt[0:128, pl.ds(base, SUB)], ds, preferred_element_type=f32
                    )
            return top, o, dqt

        top, o, dqt = lax.fori_loop(
            0, span, body,
            (
                jnp.full((8, L), -jnp.inf, f32),
                jnp.zeros((144, L), f32),
                jnp.zeros((128, L), f32),
            ),
        )
        if 2 <= t < half_tiles + 2:
            o_copy(t - 2).start()
        if 3 <= t < half_tiles + 3:
            dq_copy(t - 3).start()
        if do3:
            scale = invs[t - 2] * (1.0 / math.sqrt(HDIM))
            out = join_heads(dqt * scale).astype(bf)
            if t - 2 < half_tiles:
                dq_send[(t - 2) * F : (t - 1) * F, :] = out
            else:
                dq_own[(t - 2 - half_tiles) * F : (t - 1 - half_tiles) * F, :] = out
        if do2:
            inv = 1.0 / o[128:129]
            o = o[0:128] * inv
            out = join_heads(o).astype(bf)
            if t - 1 < half_tiles:
                o_send[(t - 1) * F : t * F, :] = out
            else:
                og[c, (t - 1 - half_tiles) * F : (t - half_tiles) * F, own_cols] = out
            grad = jnp.concatenate(split_heads(frames(gp, t - 1)), axis=0).astype(f32).T
            deltas[t - 1] = jnp.broadcast_to(jnp.sum(o * grad, axis=0, keepdims=True), (8, L))
            invs[t - 1] = inv
        if do1:
            tops[t] = jnp.broadcast_to(jnp.max(top, axis=0, keepdims=True), (8, L))

    o_far = send(og.at[c], og.at[c], (fs.at[0], fs.at[1]), clip=far)
    o_near = send(og.at[c], og.at[c], (fs.at[2], fs.at[3]), clip=near)
    o_relay = send(og.at[far], og.at[far], (fs.at[4], fs.at[5]), clip=near)
    put_dq = pltpu.make_async_copy(dq_own, dq.at[:, own_cols], os_.at[13])

    def ahead(d):
        return lax.rem(me + lax.rem(13 * d, shards), shards)

    def behind(d):
        return lax.rem(me + shards - lax.rem(13 * d, shards), shards)

    def part_copy(d, src):
        target = ahead(d)
        return send(
            wg.at[lax.div(target, 2), lax.rem(target, 2)], got.at[me],
            (ss.at[d], sr.at[src]), tm=target,
        )

    def spot_of_sum():
        at = pl.multiple_of(lax.div(me, 2) * part_rows, part_rows)
        col = pl.multiple_of(half * part_cols, 128)
        return wsum.at[pl.ds(at, part_rows), pl.ds(col, part_cols)]

    def sum_copy(d, src):
        return send(red, spot_of_sum(), (gs.at[d], gr.at[src]), tm=ahead(d))

    for t in range(half_tiles):
        o_copy(t).wait_recv()
    turned = og[c].T
    for j in range(groups):
        part = jnp.dot(turned, cotv[j], preferred_element_type=f32).astype(bf)
        lanes = (j * wide) % part_cols
        wg[:, (j * wide) // part_cols, :, lanes : lanes + wide] = part.reshape(
            shards // 2, part_rows, wide
        )
    put_dq.start()

    def start(d, carry):
        part_copy(d, me).start()
        return carry

    lax.fori_loop(1, shards, start, 0)
    o_far.start()
    o_near.start()
    got[pl.ds(me, 1)] = wg[lax.div(me, 2), pl.ds(half, 1)]

    def arrive(d, carry):
        part_copy(d, behind(d)).wait_recv()
        return carry

    lax.fori_loop(1, shards, arrive, 0)

    def add(s, acc):
        return acc + got[s].astype(f32)

    red[...] = lax.fori_loop(0, shards, add, jnp.zeros(red.shape, f32)).astype(bf)
    o_far.wait_recv()
    o_relay.start()

    def start_sum(d, carry):
        sum_copy(d, me).start()
        return carry

    lax.fori_loop(1, shards, start_sum, 0)
    put = pltpu.make_async_copy(red, spot_of_sum(), os_.at[14])
    put.start()
    o_near.wait_recv()
    o_relay.wait_recv()
    for d in range(1, groups):
        w_copy(d, lax.rem(c + groups - d, groups)).wait()
    total = jnp.zeros((rows_here, wide), f32)
    for j in range(groups):
        total += jnp.dot(og[j], wcols[j], preferred_element_type=f32)
    joined[...] = total.astype(bf)
    for t in range(half_tiles):
        o_copy(t).wait_send()
        dq_copy(t).wait()

    def end(d, carry):
        part_copy(d, behind(d)).wait_send()
        sum_copy(d, behind(d)).wait()
        return carry

    lax.fori_loop(1, shards, end, 0)
    put.wait()
    put_dq.wait()
    o_far.wait_send()
    o_near.wait_send()
    o_relay.wait_send()
    cot_far.wait_send()
    cot_near.wait_send()
    cot_relay.wait_send()
    q_copy.wait_send()
    b_copy.wait_send()
    g_copy.wait_send()

    def drain(d, carry):
        for copy in key_copies(lax.rem(me + d, shards), d, me):
            copy.wait_send()
        return carry

    def drain_halos(s, carry):
        for copy in halo_copies(s):
            copy.wait_send()
        return carry

    lax.fori_loop(1, shards, drain, 0)
    lax.fori_loop(0, shards, drain_halos, 0)


def step(tk, tv, sq, cot, ow, starts, ends, order, shards, groups):
    bf = jnp.bfloat16
    f32 = jnp.float32
    rows, wide = sq.shape
    piece = tk.shape[1]
    side = shards * piece
    window = 4 * side
    reach = side // TBLK
    L = 2 * F
    tiles = 2 * rows // F
    keys = (2 * reach + F // SBLK) * TBLK
    cols = groups * wide
    pr, pc = wide // (shards // 2), cols // 2
    dma = pltpu.SemaphoreType.DMA
    vmem = pl.BlockSpec(memory_space=pltpu.VMEM)
    return pl.pallas_call(
        functools.partial(step_kernel, shards, tiles),
        out_shape=(
            jax.ShapeDtypeStruct((rows, wide), bf),
            jax.ShapeDtypeStruct((rows, wide), bf),
            jax.ShapeDtypeStruct((wide, cols), bf),
        ),
        in_specs=[ANY] * 5 + [vmem] * 2 + [ANY],
        out_specs=(vmem, ANY, ANY),
        scratch_shapes=[
            pltpu.VMEM((2, shards, piece, 256), bf),
            pltpu.VMEM((shards, piece, 256), bf),
            pltpu.VMEM((shards, piece, 256), bf),
            pltpu.VMEM((window // 128, 128), jnp.int32),
            pltpu.VMEM((GROUP, side), bf),
            pltpu.VMEM((window, 384), bf),
            pltpu.VMEM((272, window), bf),
        ]
        + [pltpu.VMEM((keys, L), f32)] * 5
        + [pltpu.VMEM((keys, L), bf)] * 2
        + [
            pltpu.VMEM((L, 256), bf),
            pltpu.VMEM((L, 128), bf),
            pltpu.VMEM((groups, rows, wide), bf),
            pltpu.VMEM((wide, cols), bf),
            pltpu.VMEM((groups, wide, wide), bf),
            pltpu.VMEM((2, rows, 128), bf),
            pltpu.VMEM((2, rows, 128), bf),
            pltpu.VMEM((2, rows, 128), bf),
            pltpu.VMEM((8, 128), jnp.int32),
            pltpu.VMEM((2, 8, 128), jnp.int32),
            pltpu.SMEM((2, 8, 128), jnp.int32),
            pltpu.VMEM((rows, 128), bf),
            pltpu.VMEM((rows, 128), bf),
            pltpu.VMEM((rows, 128), bf),
            pltpu.VMEM((groups, rows, wide), bf),
            pltpu.VMEM((shards // 2, 2, pr, pc), bf),
            pltpu.VMEM((shards, pr, pc), bf),
            pltpu.VMEM((pr, pc), bf),
        ]
        + [dma((shards,))] * 12
        + [dma((tiles // 2,))] * 4
        + [dma((groups,))] * 2
        + [dma((6,))] * 3
        + [dma((15,))],
        compiler_params=pltpu.CompilerParams(
            collective_id=0, has_side_effects=True, vmem_limit_bytes=67043328
        ),
        name="step",
    )(tk, tv, sq, cot, ow, starts, ends, order)


def settle_kernel(joined, dq, wsum, joined_out, dq_out, w_out):
    joined_out[...] = joined[...]
    dq_out[...] = dq[...]
    w_out[...] = wsum[...].astype(jnp.float32)


def settle(joined, dq, wsum):
    steps = 2
    arrays = (joined, dq, wsum)
    specs = [
        pl.BlockSpec((x.shape[0] // steps, x.shape[1]), lambda i: (i, 0)) for x in arrays
    ]
    return pl.pallas_call(
        settle_kernel,
        grid=(steps,),
        in_specs=specs,
        out_specs=tuple(specs),
        out_shape=(
            jax.ShapeDtypeStruct(joined.shape, joined.dtype),
            jax.ShapeDtypeStruct(dq.shape, dq.dtype),
            jax.ShapeDtypeStruct(wsum.shape, jnp.float32),
        ),
        name="settle",
    )(joined, dq, wsum)


def on_device(
    student_query,
    teacher_key,
    teacher_value,
    clip_order,
    band_start,
    band_end,
    output_weight,
    cotangent,
):
    shards = lax.axis_size("tm")
    groups = lax.axis_size("clip")
    rows, wide = student_query.shape
    trows = teacher_key.shape[0]
    piece = trows // shards
    blocks = rows // SBLK

    return settle(
        *step(
            teacher_key.reshape(shards, piece, wide),
            teacher_value.reshape(shards, piece, wide),
            student_query, cotangent, output_weight,
            band_start.reshape(1, blocks), band_end.reshape(1, blocks),
            clip_order.reshape(-1, 128), shards, groups,
        )
    )


def solution(mesh):
    return jax.shard_map(
        on_device,
        mesh=mesh,
        in_specs=(
            P("tm", "clip"),
            P("tm", "clip"),
            P("tm", "clip"),
            P(),
            P("tm"),
            P("tm"),
            P("clip", None),
            P("tm", "clip"),
        ),
        out_specs=(P("tm", "clip"), P("tm", "clip"), P("clip", None)),
        check_vma=False,
    )
```

profile of v0, /device:TPU:0, one launch (start us, length us, event | category | flops | bytes accessed | tf_op | source)
XLA Modules:
  0.0 121.3 jit_solution(210162330890619482)
XLA Ops:
  0.6 118.4 %step.1 = (bf16[512,256]{1,0:T(8,128)(2,1)}, bf16[512,256]{1,0:T(8,128)(2,1)}, bf16[256,1024]{1,0:T(8,128)(2,1)}) custom-call(bf16[32,64,256]{2,1,0:T(8,128)(2,1)} %bitcast.5, bf16[32,64,256]{2,1,0:T(8,128)(2,1)} %bitcast.6, bf16[512,256]{1,0:T(8,128)(2,1)} %sq.1, bf16[512,256]{1,0:T(8,128)(2,1)} %cot.1, bf16[256,1024]{1,0:T(8,128)(2,1)} %ow.1, ...), custom_call_target="tpu_custom_call" | custom-call | tf_op jit(solution)/shard_map/step/pallas_call | solution.py:511
  119.0 2.3 %settle.1 = (bf16[512,256]{1,0:T(8,128)(2,1)}, bf16[512,256]{1,0:T(8,128)(2,1)}, f32[256,1024]{1,0:T(8,128)}) custom-call(bf16[512,256]{1,0:T(8,128)(2,1)} %get-tuple-element.6.joined, bf16[512,256]{1,0:T(8,128)(2,1)} %get-tuple-element.7.dq, bf16[256,1024]{1,0:T(8,128)(2,1)} %get-tuple-element.8.wsum), custom_call_target="tpu_custom_call" | custom-call | tf_op jit(solution)/shard_map/settle/pallas_call | solution.py:575
where the time goes:
time: 122 us; the launch traced here: 121 us
  Pallas kernels  121 us (99%)
    pallas_call x1, Pallas kernels, step(): pl.pallas_call(functools.partial(step_kernel, shards, tiles), out_shape=(...  118 us

commit v1 on v0

--- a/solution.py
+++ b/solution.py
@@ -69,7 +69,7 @@
 def step_kernel(
     shards, tiles, tk, tv, sq, cot, ow, starts, ends, order,
     joined, dq, wsum,
-    kvin, left, right, idx, hot, kv, kvt, s0, s1, d0, d1, d2, p0, p1, qb, gb,
+    kvin, left, right, idx, hot, kv, kvt, s0, s1, d0, d1, d2, p0, p1, p2, p3, p4, p5, qb, gb, gb2,
     cotv, wv, wcols, gv, qp, gp, bv, bp, band,
     o_send, dq_send, dq_own, og, wg, got, red,
     ks, kr, vs, vr, ls, lr, rs, rr, ss, sr, gs, gr,
@@ -97,7 +97,7 @@
     half_tiles = tiles // 2
     reach = side // TBLK
     span = (2 * reach + nb) // per
-    scores, dprobs, weights = (s0, s1), (d0, d1, d2), (p0, p1)
+    scores, dprobs = (s0, s1), (d0, d1, d2)
     part_rows, part_cols = red.shape
     own_cols = pl.ds(pl.multiple_of(half * 128, 128), 128)
     mate_cols = pl.ds(pl.multiple_of((1 - half) * 128, 128), 128)
@@ -270,6 +270,10 @@
     flane = lax.broadcasted_iota(jnp.int32, (F, 128), 1)
     zero = jnp.zeros((F, 128), bf)
     tops, deltas, invs = {}, {}, {}
+    scale = 1.0 / math.sqrt(HDIM)
+
+    def weights(t):
+        return (p0, p1)[t % 2] if t < half_tiles else (p2, p3, p4, p5)[t - half_tiles]
 
     def tile_at(t):
         return lax.rem(t + (1 - half) * half_tiles, tiles)
@@ -300,12 +304,14 @@
             dq_send.at[part], dq.at[part, own_cols], (dss.at[t], dsr.at[t]), tm=mate
         )
 
-    for t in range(tiles + 2):
-        do1, do2, do3 = t < tiles, 1 <= t <= tiles, t >= 2
+    for t in range(tiles + 1):
+        do1, do2, do3 = t < tiles, t >= 1, 2 <= t < half_tiles + 2
+        keep = t < half_tiles
         if do1:
             q = frames(qp, t) * bf(1.0 / math.sqrt(HDIM))
             qb[0:F, 0:128], qb[F:L, 0:128] = split_heads(q)
-            gb[0:F, :], gb[F:L, :] = split_heads(frames(gp, t))
+            if keep:
+                gb[0:F, :], gb[F:L, :] = split_heads(frames(gp, t))
             block = lax.broadcasted_iota(jnp.int32, (SBLK, 128), 1)
             row = lax.div(tile_at(t), half_tiles)
             col = lax.rem(tile_at(t), half_tiles) * nb
@@ -329,20 +335,21 @@
                     s = lax.dot_general(
                         kv[pl.ds(base, SUB), 0:256], qb[...], nt, preferred_element_type=f32
                     )
-                    dprobs[t % 3][pl.ds(at, SUB), :] = lax.dot_general(
-                        kv[pl.ds(base, SUB), 256:384], gb[...], nt, preferred_element_type=f32
-                    )
+                    if keep:
+                        dprobs[t % 3][pl.ds(at, SUB), :] = lax.dot_general(
+                            kv[pl.ds(base, SUB), 256:384], gb[...], nt, preferred_element_type=f32
+                        )
                     scores[t % 2][pl.ds(at, SUB), :] = s
                     top = jnp.maximum(top, jnp.max(s.reshape(SUB // 8, 8, L), axis=0))
                 if do2:
                     base = spot(t - 1, k, u)
                     s = scores[(t - 1) % 2][pl.ds(at, SUB), :].reshape(SUB // 8, 8, L)
                     e = jnp.exp(s - tops[t - 1][None]).reshape(SUB, L).astype(bf)
-                    weights[(t - 1) % 2][pl.ds(at, SUB), :] = e
+                    weights(t - 1)[pl.ds(at, SUB), :] = e
                     o = o + jnp.dot(kvt[128:272, pl.ds(base, SUB)], e, preferred_element_type=f32)
                 if do3:
                     base = spot(t - 2, k, u)
-                    e = weights[t % 2][pl.ds(at, SUB), :].astype(f32).reshape(SUB // 8, 8, L)
+                    e = weights(t - 2)[pl.ds(at, SUB), :].astype(f32).reshape(SUB // 8, 8, L)
                     d = dprobs[(t - 2) % 3][pl.ds(at, SUB), :].reshape(SUB // 8, 8, L)
                     ds = (e * (d - deltas[t - 2][None])).reshape(SUB, L).astype(bf)
                     dqt = dqt + jnp.dot(
@@ -363,12 +370,8 @@
         if 3 <= t < half_tiles + 3:
             dq_copy(t - 3).start()
         if do3:
-            scale = invs[t - 2] * (1.0 / math.sqrt(HDIM))
-            out = join_heads(dqt * scale).astype(bf)
-            if t - 2 < half_tiles:
-                dq_send[(t - 2) * F : (t - 1) * F, :] = out
-            else:
-                dq_own[(t - 2 - half_tiles) * F : (t - 1 - half_tiles) * F, :] = out
+            out = join_heads(dqt * (invs[t - 2] * scale)).astype(bf)
+            dq_send[(t - 2) * F : (t - 1) * F, :] = out
         if do2:
             inv = 1.0 / o[128:129]
             o = o[0:128] * inv
@@ -383,6 +386,32 @@
         if do1:
             tops[t] = jnp.broadcast_to(jnp.max(top, axis=0, keepdims=True), (8, L))
 
+    def leave(first):
+        pairs = ((first, gb), (first + 1, gb2))
+        for t, ref in pairs:
+            ref[0:F, :], ref[F:L, :] = split_heads(frames(gp, t))
+
+        def body(k, carry):
+            carry = list(carry)
+            for u in range(CH // SUB):
+                at = pl.multiple_of(k * CH + u * SUB, SUB)
+                for i, (t, ref) in enumerate(pairs):
+                    base = spot(t, k, u)
+                    d = lax.dot_general(
+                        kv[pl.ds(base, SUB), 256:384], ref[...], nt, preferred_element_type=f32
+                    ).reshape(SUB // 8, 8, L)
+                    e = weights(t)[pl.ds(at, SUB), :].astype(f32).reshape(SUB // 8, 8, L)
+                    ds = (e * (d - deltas[t][None])).reshape(SUB, L).astype(bf)
+                    carry[i] = carry[i] + jnp.dot(
+                        kvt[0:128, pl.ds(base, SUB)], ds, preferred_element_type=f32
+                    )
+            return tuple(carry)
+
+        sums = lax.fori_loop(0, span, body, (jnp.zeros((128, L), f32),) * 2)
+        for (t, _), dqt in zip(pairs, sums):
+            at = (t - half_tiles) * F
+            dq_own[at : at + F, :] = join_heads(dqt * (invs[t] * scale)).astype(bf)
+
     o_far = send(og.at[c], og.at[c], (fs.at[0], fs.at[1]), clip=far)
     o_near = send(og.at[c], og.at[c], (fs.at[2], fs.at[3]), clip=near)
     o_relay = send(og.at[far], og.at[far], (fs.at[4], fs.at[5]), clip=near)
@@ -418,7 +447,6 @@
         wg[:, (j * wide) // part_cols, :, lanes : lanes + wide] = part.reshape(
             shards // 2, part_rows, wide
         )
-    put_dq.start()
 
     def start(d, carry):
         part_copy(d, me).start()
@@ -428,6 +456,7 @@
     o_far.start()
     o_near.start()
     got[pl.ds(me, 1)] = wg[lax.div(me, 2), pl.ds(half, 1)]
+    leave(half_tiles)
 
     def arrive(d, carry):
         part_copy(d, behind(d)).wait_recv()
@@ -449,6 +478,7 @@
     lax.fori_loop(1, shards, start_sum, 0)
     put = pltpu.make_async_copy(red, spot_of_sum(), os_.at[14])
     put.start()
+    leave(half_tiles + 2)
     o_near.wait_recv()
     o_relay.wait_recv()
     for d in range(1, groups):
@@ -457,6 +487,7 @@
     for j in range(groups):
         total += jnp.dot(og[j], wcols[j], preferred_element_type=f32)
     joined[...] = total.astype(bf)
+    put_dq.start()
     for t in range(half_tiles):
         o_copy(t).wait_send()
         dq_copy(t).wait()
@@ -527,9 +558,10 @@
             pltpu.VMEM((272, window), bf),
         ]
         + [pltpu.VMEM((keys, L), f32)] * 5
-        + [pltpu.VMEM((keys, L), bf)] * 2
+        + [pltpu.VMEM((keys, L), bf)] * 6
         + [
             pltpu.VMEM((L, 256), bf),
+            pltpu.VMEM((L, 128), bf),
             pltpu.VMEM((L, 128), bf),
             pltpu.VMEM((groups, rows, wide), bf),
             pltpu.VMEM((wide, cols), bf),

time: 122 us -> 117 us (0.959)
  Pallas kernels: 121 us -> 115 us
    pallas_call x1, Pallas kernels: 118 us -> 113 us  [step(): pl.pallas_call(functools.partial(step_kernel, shards, tiles), out_shape=(...]
where the time goes in v1:
time: 117 us; the launch traced here: 116 us
  Pallas kernels  115 us (98%)
    pallas_call x1, Pallas kernels, step(): pl.pallas_call(functools.partial(step_kernel, shards, tiles), out_shape=(...  113 us

profile of v1, /device:TPU:0, one launch (start us, length us, event | category | flops | bytes accessed | tf_op | source)
XLA Modules:
  0.0 116.1 jit_solution(63928415854717953)
XLA Ops:
  0.6 113.2 %step.1 = (bf16[512,256]{1,0:T(8,128)(2,1)}, bf16[512,256]{1,0:T(8,128)(2,1)}, bf16[256,1024]{1,0:T(8,128)(2,1)}) custom-call(bf16[32,64,256]{2,1,0:T(8,128)(2,1)} %bitcast.5, bf16[32,64,256]{2,1,0:T(8,128)(2,1)} %bitcast.6, bf16[512,256]{1,0:T(8,128)(2,1)} %sq.1, bf16[512,256]{1,0:T(8,128)(2,1)} %cot.1, bf16[256,1024]{1,0:T(8,128)(2,1)} %ow.1, ...), custom_call_target="tpu_custom_call" | custom-call | tf_op jit(solution)/shard_map/step/pallas_call | solution.py:542
  113.8 2.3 %settle.1 = (bf16[512,256]{1,0:T(8,128)(2,1)}, bf16[512,256]{1,0:T(8,128)(2,1)}, f32[256,1024]{1,0:T(8,128)}) custom-call(bf16[512,256]{1,0:T(8,128)(2,1)} %get-tuple-element.6.joined, bf16[512,256]{1,0:T(8,128)(2,1)} %get-tuple-element.7.dq, bf16[256,1024]{1,0:T(8,128)(2,1)} %get-tuple-element.8.wsum), custom_call_target="tpu_custom_call" | custom-call | tf_op jit(solution)/shard_map/settle/pallas_call | solution.py:607

commit v2 on v1

--- a/solution.py
+++ b/solution.py
@@ -69,7 +69,7 @@
 def step_kernel(
     shards, tiles, tk, tv, sq, cot, ow, starts, ends, order,
     joined, dq, wsum,
-    kvin, left, right, idx, hot, kv, kvt, s0, s1, d0, d1, d2, p0, p1, p2, p3, p4, p5, qb, gb, gb2,
+    kvin, left, right, idx, hot, kv, kvt, s0, s1, p0, p1, p2, p3, p4, p5, qb, gb, gb2,
     cotv, wv, wcols, gv, qp, gp, bv, bp, band,
     o_send, dq_send, dq_own, og, wg, got, red,
     ks, kr, vs, vr, ls, lr, rs, rr, ss, sr, gs, gr,
@@ -97,7 +97,7 @@
     half_tiles = tiles // 2
     reach = side // TBLK
     span = (2 * reach + nb) // per
-    scores, dprobs = (s0, s1), (d0, d1, d2)
+    scores = (s0, s1)
     part_rows, part_cols = red.shape
     own_cols = pl.ds(pl.multiple_of(half * 128, 128), 128)
     mate_cols = pl.ds(pl.multiple_of((1 - half) * 128, 128), 128)
@@ -141,15 +141,14 @@
     b_copy = send(bv, bp.at[half], (ms.at[2], ms.at[3]), tm=mate)
     g_copy = send(gv.at[1 - half], gp.at[half], (ms.at[4], ms.at[5]), tm=mate)
 
-    cot_far.start()
-    cot_near.start()
-
     def start_keys(d, carry):
         for copy in key_copies(lax.rem(me + d, shards), d, me):
             copy.start()
         return carry
 
     lax.fori_loop(1, shards, start_keys, 0)
+    cot_far.start()
+    cot_near.start()
     q_copy.start()
     b_copy.start()
     mine_kv = (
@@ -179,12 +178,77 @@
     ) + tuple(get_idx)
     for copy in mine_cot + mine_kv + mine_rest:
         copy.start()
-    for copy in mine_cot + mine_kv:
+    for copy in mine_kv:
         copy.wait()
     for copy in halo_copies(me):
         copy.start()
+    for copy in mine_rest:
+        copy.wait()
+
+    def choose(slot, first):
+        for r in range(GROUP // 128):
+            one_hot_rows(
+                idx[pl.ds(first + r, 1), :], hot.at[slot], r * 128, side, piece
+            )
+
+    def place(slot, src, first):
+        rows = jnp.dot(
+            hot[slot], src.reshape(side, 256), preferred_element_type=f32
+        ).astype(bf)
+        at = pl.multiple_of(first, GROUP)
+        kv[pl.ds(at, GROUP), 0:128] = rows[:, 0:128]
+        kv[pl.ds(at, GROUP), 256:384] = rows[:, 128:256]
+        kvt[0:256, pl.ds(at, GROUP)] = rows.T
+
+    slots = 2 * side // GROUP
+    each = GROUP // 128
+
+    def choose_own(j, carry):
+        choose(j, irows + j * each)
+        return carry
+
+    def choose_halo(j, carry):
+        choose(j, j * each + 2 * irows * lax.div(2 * j, slots))
+        return carry
+
+    def sort_own(j, carry):
+        place(j, kvin[lax.div(2 * j, slots)], side + j * GROUP)
+        return carry
+
+    def sort_left(j, carry):
+        place(j, left[...], j * GROUP)
+        return carry
+
+    def sort_right(j, carry):
+        place(j, right[...], j * GROUP + 2 * side)
+        return carry
+
+    def forward(d, carry):
+        s = lax.rem(me + shards - d, shards)
+        for copy in key_copies(lax.rem(me + d, shards), d, s):
+            copy.wait_recv()
+        for copy in halo_copies(s):
+            copy.start()
+        return carry
+
+    lax.fori_loop(0, slots, choose_own, 0)
+    lax.fori_loop(1, 3, forward, 0)
+    kvt[256:272, :] = jnp.ones((16, kvt.shape[1]), bf)
+    lane = lax.broadcasted_iota(jnp.int32, (128, 128), 1)
+
+    def mark(k, carry):
+        at = pl.multiple_of(k * TBLK, TBLK)
+        kv[pl.ds(at, TBLK), 128:256] = jnp.where(lane == k, 1.0, 0.0).astype(bf)
+        return carry
+
+    lax.fori_loop(0, 4 * reach, mark, 0)
+    lax.fori_loop(3, shards, forward, 0)
+    lax.fori_loop(0, slots, sort_own, 0)
     cot_far.wait_recv()
     cot_relay.start()
+    lax.fori_loop(0, slots, choose_halo, 0)
+    for copy in mine_cot:
+        copy.wait()
     cot_near.wait_recv()
     cot_relay.wait_recv()
     nt = (((1,), (1,)), ((), ()))
@@ -196,76 +260,28 @@
     gv[0] = grad[:, 0:128].astype(bf)
     gv[1] = grad[:, 128:256].astype(bf)
 
-    def forward(d, carry):
-        s = lax.rem(me + shards - d, shards)
-        for copy in key_copies(lax.rem(me + d, shards), d, s):
-            copy.wait_recv()
-        for copy in halo_copies(s):
-            copy.start()
-        return carry
-
-    lax.fori_loop(1, 3, forward, 0)
+    def came_left(s, carry):
+        halo_copies(s)[1].wait_recv()
+        return carry
+
+    def came_right(s, carry):
+        halo_copies(s)[0].wait_recv()
+        return carry
+
+    lax.fori_loop(0, shards, came_left, 0)
+    lax.fori_loop(0, slots // 2, sort_left, 0)
     g_copy.start()
     put_g = pltpu.make_async_copy(gv.at[half], gp.at[half], os_.at[11])
     put_g.start()
-    for copy in mine_rest:
-        copy.wait()
-    kvt[256:272, :] = jnp.ones((16, kvt.shape[1]), bf)
-    lane = lax.broadcasted_iota(jnp.int32, (128, 128), 1)
-
-    def mark(k, carry):
-        at = pl.multiple_of(k * TBLK, TBLK)
-        kv[pl.ds(at, TBLK), 128:256] = jnp.where(lane == k, 1.0, 0.0).astype(bf)
-        return carry
-
-    lax.fori_loop(0, 4 * reach, mark, 0)
-    lax.fori_loop(3, shards, forward, 0)
     for d in range(1, groups):
         w_copy(d, c).start()
-
-    def place(src, first, j):
-        for r in range(GROUP // 128):
-            row = lax.div(first, 128) + j * (GROUP // 128) + r
-            one_hot_rows(idx[pl.ds(row, 1), :], hot, r * 128, side, piece)
-        rows = jnp.dot(hot[...], src.reshape(side, 256), preferred_element_type=f32).astype(bf)
-        at = pl.multiple_of(first + j * GROUP, GROUP)
-        kv[pl.ds(at, GROUP), 0:128] = rows[:, 0:128]
-        kv[pl.ds(at, GROUP), 256:384] = rows[:, 128:256]
-        kvt[0:256, pl.ds(at, GROUP)] = rows.T
-
-    def sort_own(j, carry):
-        place(kvin[lax.div(j * GROUP, side)], side, j)
-        return carry
-
-    def sort_left(j, carry):
-        place(left[...], 0, j)
-        return carry
-
-    def sort_right(j, carry):
-        place(right[...], 3 * side, j)
-        return carry
-
-    lax.fori_loop(0, 2 * side // GROUP, sort_own, 0)
+    lax.fori_loop(0, shards, came_right, 0)
+    lax.fori_loop(slots // 2, slots, sort_right, 0)
     q_copy.wait_recv()
     b_copy.wait_recv()
-    g_copy.wait_recv()
-    put_g.wait()
     get_band = pltpu.make_async_copy(bp, band, os_.at[12])
     get_band.start()
     get_band.wait()
-
-    def came_left(s, carry):
-        halo_copies(s)[1].wait_recv()
-        return carry
-
-    def came_right(s, carry):
-        halo_copies(s)[0].wait_recv()
-        return carry
-
-    lax.fori_loop(0, shards, came_left, 0)
-    lax.fori_loop(0, side // GROUP, sort_left, 0)
-    lax.fori_loop(0, shards, came_right, 0)
-    lax.fori_loop(0, side // GROUP, sort_right, 0)
 
     flane = lax.broadcasted_iota(jnp.int32, (F, 128), 1)
     zero = jnp.zeros((F, 128), bf)
@@ -306,12 +322,11 @@
 
     for t in range(tiles + 1):
         do1, do2, do3 = t < tiles, t >= 1, 2 <= t < half_tiles + 2
-        keep = t < half_tiles
+        if do3:
+            gb[0:F, :], gb[F:L, :] = split_heads(frames(gp, t - 2))
         if do1:
             q = frames(qp, t) * bf(1.0 / math.sqrt(HDIM))
             qb[0:F, 0:128], qb[F:L, 0:128] = split_heads(q)
-            if keep:
-                gb[0:F, :], gb[F:L, :] = split_heads(frames(gp, t))
             block = lax.broadcasted_iota(jnp.int32, (SBLK, 128), 1)
             row = lax.div(tile_at(t), half_tiles)
             col = lax.rem(tile_at(t), half_tiles) * nb
@@ -335,10 +350,6 @@
                     s = lax.dot_general(
                         kv[pl.ds(base, SUB), 0:256], qb[...], nt, preferred_element_type=f32
                     )
-                    if keep:
-                        dprobs[t % 3][pl.ds(at, SUB), :] = lax.dot_general(
-                            kv[pl.ds(base, SUB), 256:384], gb[...], nt, preferred_element_type=f32
-                        )
                     scores[t % 2][pl.ds(at, SUB), :] = s
                     top = jnp.maximum(top, jnp.max(s.reshape(SUB // 8, 8, L), axis=0))
                 if do2:
@@ -350,7 +361,9 @@
                 if do3:
                     base = spot(t - 2, k, u)
                     e = weights(t - 2)[pl.ds(at, SUB), :].astype(f32).reshape(SUB // 8, 8, L)
-                    d = dprobs[(t - 2) % 3][pl.ds(at, SUB), :].reshape(SUB // 8, 8, L)
+                    d = lax.dot_general(
+                        kv[pl.ds(base, SUB), 256:384], gb[...], nt, preferred_element_type=f32
+                    ).reshape(SUB // 8, 8, L)
                     ds = (e * (d - deltas[t - 2][None])).reshape(SUB, L).astype(bf)
                     dqt = dqt + jnp.dot(
                         kvt[0:128, pl.ds(base, SUB)], ds, preferred_element_type=f32
@@ -365,6 +378,9 @@
                 jnp.zeros((128, L), f32),
             ),
         )
+        if t == 1:
+            g_copy.wait_recv()
+            put_g.wait()
         if 2 <= t < half_tiles + 2:
             o_copy(t - 2).start()
         if 3 <= t < half_tiles + 3:
@@ -553,11 +569,11 @@
             pltpu.VMEM((shards, piece, 256), bf),
             pltpu.VMEM((shards, piece, 256), bf),
             pltpu.VMEM((window // 128, 128), jnp.int32),
-            pltpu.VMEM((GROUP, side), bf),
+            pltpu.VMEM((2 * side // GROUP, GROUP, side), bf),
             pltpu.VMEM((window, 384), bf),
             pltpu.VMEM((272, window), bf),
         ]
-        + [pltpu.VMEM((keys, L), f32)] * 5
+        + [pltpu.VMEM((keys, L), f32)] * 2
         + [pltpu.VMEM((keys, L), bf)] * 6
         + [
             pltpu.VMEM((L, 256), bf),

time: 117 us -> 121 us (1.034)
  Pallas kernels: 115 us -> 119 us
    pallas_call x1, Pallas kernels: 113 us -> 117 us  [step(): pl.pallas_call(functools.partial(step_kernel, shards, tiles), out_shape=(...]
where the time goes in v2:
time: 121 us; the launch traced here: 120 us
  Pallas kernels  119 us (98%)
    pallas_call x1, Pallas kernels, step(): pl.pallas_call(functools.partial(step_kernel, shards, tiles), out_shape=(...  117 us

profile of v2, /device:TPU:0, one launch (start us, length us, event | category | flops | bytes accessed | tf_op | source)
XLA Modules:
  0.0 119.6 jit_solution(6933402191118181895)
XLA Ops:
  0.6 116.7 %step.1 = (bf16[512,256]{1,0:T(8,128)(2,1)}, bf16[512,256]{1,0:T(8,128)(2,1)}, bf16[256,1024]{1,0:T(8,128)(2,1)}) custom-call(bf16[32,64,256]{2,1,0:T(8,128)(2,1)} %bitcast.5, bf16[32,64,256]{2,1,0:T(8,128)(2,1)} %bitcast.6, bf16[512,256]{1,0:T(8,128)(2,1)} %sq.1, bf16[512,256]{1,0:T(8,128)(2,1)} %cot.1, bf16[256,1024]{1,0:T(8,128)(2,1)} %ow.1, ...), custom_call_target="tpu_custom_call" | custom-call | tf_op jit(solution)/shard_map/step/pallas_call | solution.py:558
  117.3 2.3 %settle.1 = (bf16[512,256]{1,0:T(8,128)(2,1)}, bf16[512,256]{1,0:T(8,128)(2,1)}, f32[256,1024]{1,0:T(8,128)}) custom-call(bf16[512,256]{1,0:T(8,128)(2,1)} %get-tuple-element.6.joined, bf16[512,256]{1,0:T(8,128)(2,1)} %get-tuple-element.7.dq, bf16[256,1024]{1,0:T(8,128)(2,1)} %get-tuple-element.8.wsum), custom_call_target="tpu_custom_call" | custom-call | tf_op jit(solution)/shard_map/settle/pallas_call | solution.py:623

commit v3 on v2

--- a/solution.py
+++ b/solution.py
@@ -141,14 +141,15 @@
     b_copy = send(bv, bp.at[half], (ms.at[2], ms.at[3]), tm=mate)
     g_copy = send(gv.at[1 - half], gp.at[half], (ms.at[4], ms.at[5]), tm=mate)
 
+    cot_far.start()
+    cot_near.start()
+
     def start_keys(d, carry):
         for copy in key_copies(lax.rem(me + d, shards), d, me):
             copy.start()
         return carry
 
     lax.fori_loop(1, shards, start_keys, 0)
-    cot_far.start()
-    cot_near.start()
     q_copy.start()
     b_copy.start()
     mine_kv = (
@@ -231,22 +232,8 @@
             copy.start()
         return carry
 
-    lax.fori_loop(0, slots, choose_own, 0)
-    lax.fori_loop(1, 3, forward, 0)
-    kvt[256:272, :] = jnp.ones((16, kvt.shape[1]), bf)
-    lane = lax.broadcasted_iota(jnp.int32, (128, 128), 1)
-
-    def mark(k, carry):
-        at = pl.multiple_of(k * TBLK, TBLK)
-        kv[pl.ds(at, TBLK), 128:256] = jnp.where(lane == k, 1.0, 0.0).astype(bf)
-        return carry
-
-    lax.fori_loop(0, 4 * reach, mark, 0)
-    lax.fori_loop(3, shards, forward, 0)
-    lax.fori_loop(0, slots, sort_own, 0)
     cot_far.wait_recv()
     cot_relay.start()
-    lax.fori_loop(0, slots, choose_halo, 0)
     for copy in mine_cot:
         copy.wait()
     cot_near.wait_recv()
@@ -260,19 +247,34 @@
     gv[0] = grad[:, 0:128].astype(bf)
     gv[1] = grad[:, 128:256].astype(bf)
 
-    def came_left(s, carry):
-        halo_copies(s)[1].wait_recv()
-        return carry
-
-    def came_right(s, carry):
-        halo_copies(s)[0].wait_recv()
-        return carry
-
-    lax.fori_loop(0, shards, came_left, 0)
-    lax.fori_loop(0, slots // 2, sort_left, 0)
+    lax.fori_loop(1, 3, forward, 0)
     g_copy.start()
     put_g = pltpu.make_async_copy(gv.at[half], gp.at[half], os_.at[11])
     put_g.start()
+    kvt[256:272, :] = jnp.ones((16, kvt.shape[1]), bf)
+    lane = lax.broadcasted_iota(jnp.int32, (128, 128), 1)
+
+    def mark(k, carry):
+        at = pl.multiple_of(k * TBLK, TBLK)
+        kv[pl.ds(at, TBLK), 128:256] = jnp.where(lane == k, 1.0, 0.0).astype(bf)
+        return carry
+
+    lax.fori_loop(0, 4 * reach, mark, 0)
+    lax.fori_loop(3, shards, forward, 0)
+    lax.fori_loop(0, slots, choose_own, 0)
+    lax.fori_loop(0, slots, sort_own, 0)
+    lax.fori_loop(0, slots, choose_halo, 0)
+
+    def came_left(s, carry):
+        halo_copies(s)[1].wait_recv()
+        return carry
+
+    def came_right(s, carry):
+        halo_copies(s)[0].wait_recv()
+        return carry
+
+    lax.fori_loop(0, shards, came_left, 0)
+    lax.fori_loop(0, slots // 2, sort_left, 0)
     for d in range(1, groups):
         w_copy(d, c).start()
     lax.fori_loop(0, shards, came_right, 0)

time: 121 us -> 119 us (0.983); the launches traced: 120 us -> 119 us
  no operation moved by 1% of the time
where the time goes in v3:
time: 119 us
  Pallas kernels  118 us (99%)
    pallas_call x1, Pallas kernels, step(): pl.pallas_call(functools.partial(step_kernel, shards, tiles), out_shape=(...  116 us

profile of v3, /device:TPU:0, one launch (start us, length us, event | category | flops | bytes accessed | tf_op | source)
XLA Modules:
  0.0 118.9 jit_solution(15486261072533340956)
XLA Ops:
  0.6 115.9 %step.1 = (bf16[512,256]{1,0:T(8,128)(2,1)}, bf16[512,256]{1,0:T(8,128)(2,1)}, bf16[256,1024]{1,0:T(8,128)(2,1)}) custom-call(bf16[32,64,256]{2,1,0:T(8,128)(2,1)} %bitcast.5, bf16[32,64,256]{2,1,0:T(8,128)(2,1)} %bitcast.6, bf16[512,256]{1,0:T(8,128)(2,1)} %sq.1, bf16[512,256]{1,0:T(8,128)(2,1)} %cot.1, bf16[256,1024]{1,0:T(8,128)(2,1)} %ow.1, ...), custom_call_target="tpu_custom_call" | custom-call | tf_op jit(solution)/shard_map/step/pallas_call | solution.py:560
  116.6 2.3 %settle.1 = (bf16[512,256]{1,0:T(8,128)(2,1)}, bf16[512,256]{1,0:T(8,128)(2,1)}, f32[256,1024]{1,0:T(8,128)}) custom-call(bf16[512,256]{1,0:T(8,128)(2,1)} %get-tuple-element.6.joined, bf16[512,256]{1,0:T(8,128)(2,1)} %get-tuple-element.7.dq, bf16[256,1024]{1,0:T(8,128)(2,1)} %get-tuple-element.8.wsum), custom_call_target="tpu_custom_call" | custom-call | tf_op jit(solution)/shard_map/settle/pallas_call | solution.py:625
